TPU v7x, 256 devices: a whole 4x4x8 slice. The times are simulated.
256 devices in a mesh: leaf: 32 (over x_hi, z, core), head: 8 (over x_lo, y).
Axes of the slice: x: 4 (x_hi: 2, x_lo: 2; x = x_hi * 2 + x_lo), y: 4, z: 8, core: 2. Of those that a mesh axis runs over, the one named last changes fastest.
Arguments:
- latents: bfloat16 [2048, 512], P('leaf'), may hold values from -14 to 14
- queries: bfloat16 [4096, 64, 128], P('leaf', 'head'), may hold values from -14 to 14
- grad_out: bfloat16 [4096, 64, 128], P('leaf', 'head'), may hold values from -6 to 6
- key_up_matrix: bfloat16 [64, 128, 512], P('head'), may hold values from -0.25 to 0.25
- value_up_matrix: bfloat16 [64, 512, 128], P('head'), may hold values from -0.25 to 0.25
- parents: int32 [256], replicated, may hold values from 0 to 254, as said below
- branch_node: int32 [32, 8], P('leaf'), may hold values from 0 to 255
- branch_lengths: int32 [32, 8], P('leaf'), may hold values from 1 to 40, 128 in all within a row
Outputs:
- d_queries: bfloat16 [4096, 64, 128], P('leaf', 'head')
- d_latents: float32 [2048, 512], P('leaf')
Inputs may be any that keep to these rules, and one draw needn't show every extreme that they name: parents[0] = 0 and parents[n] < n for every n >= 1.
All inputs are finite; a program needn't handle non-finite values.
Results may differ from a plain program's by a relative error of at most 0.025.
The roundings to bfloat16 on the way count: a program that leaves them out, or rounds other values in their place, can miss the bound.
Values may be sent and summed in bfloat16 or wider, within the bound.
A program may use at most 64 MiB of HBM per device.

v0:
```python
import jax
import jax.numpy as jnp
from jax import lax
from jax.sharding import PartitionSpec as P

NODE_LEN = 8


softmax_scale = 192.0 ** (-0.5)
masked_score = -1e30


def ancestry(parents):
    node_count = parents.shape[0]
    indices = jnp.arange(node_count, dtype=jnp.int32)
    linked = (parents[:, None] == indices[None, :]) | (indices[:, None] == indices[None, :])
    closure = linked.astype(jnp.float32)
    for squaring in range(node_count.bit_length()):
        closure = jnp.minimum(jnp.dot(closure, closure, precision=lax.Precision.HIGHEST), 1.0)
    return closure


def token_nodes(lengths_row, nodes_row, tok_count):
    bounds = jnp.cumsum(lengths_row)
    places = jnp.arange(tok_count, dtype=jnp.int32)
    branch_of = jnp.sum((places[:, None] >= bounds[None, :]).astype(jnp.int32), axis=1)
    select = branch_of[:, None] == jnp.arange(lengths_row.shape[0], dtype=jnp.int32)[None, :]
    return jnp.sum(jnp.where(select, nodes_row[None, :], 0), axis=1)


def live_keys(node_list, closure):
    node_count = closure.shape[0]
    select = (node_list[:, None] == jnp.arange(node_count, dtype=jnp.int32)[None, :]).astype(
        jnp.float32
    )
    reached = jnp.dot(select, closure, precision=lax.Precision.HIGHEST) > 0.5
    return jnp.repeat(reached, NODE_LEN, axis=1)


def on_device(
    latents, queries, grad_out, key_up_matrix, value_up_matrix, parents, branch_node, branch_lengths
):
    closure = ancestry(parents)
    tok_count = queries.shape[0]
    heads_here = queries.shape[1]
    width = latents.shape[1]
    node_list = token_nodes(branch_lengths[0], branch_node[0], tok_count)
    key_live = live_keys(node_list, closure)
    prefix_rows = key_live.shape[1]
    query_latent = jnp.einsum(
        "thd,hdc->thc", queries, key_up_matrix, preferred_element_type=jnp.float32
    ).astype(jnp.bfloat16)
    grad_latent = jnp.einsum(
        "thv,hcv->thc", grad_out, value_up_matrix, preferred_element_type=jnp.float32
    ).astype(jnp.bfloat16)

    def scores(block_keys):
        usable = key_live[:, None, :]
        scaled = (
            jnp.einsum("thc,kc->thk", query_latent, block_keys, preferred_element_type=jnp.float32)
            * softmax_scale
        )
        return (usable, jnp.where(usable, scaled, masked_score))

    forward_start = (
        jnp.full((tok_count, heads_here), masked_score, jnp.float32),
        jnp.zeros((tok_count, heads_here), jnp.float32),
        jnp.zeros((tok_count, heads_here, width), jnp.float32),
    )
    block_keys = lax.all_gather(latents, "leaf", axis=0, tiled=True)

    def advance(state):
        running_max, running_sum, weighted = state
        usable, logits = scores(block_keys)
        new_max = jnp.maximum(running_max, jnp.max(logits, axis=-1))
        weights = jnp.where(usable, jnp.exp(logits - new_max[..., None]), 0.0)
        weighted = jnp.einsum(
            "thk,kc->thc",
            weights.astype(jnp.bfloat16),
            block_keys,
            preferred_element_type=jnp.float32,
        )
        return (new_max, jnp.sum(weights, axis=-1), weighted)

    running_max, running_sum, weighted = advance(forward_start)
    attended = weighted / running_sum[..., None]
    log_norm = running_max + jnp.log(running_sum)
    delta = jnp.sum(grad_latent.astype(jnp.float32) * attended, axis=-1)
    backward_start = (
        jnp.zeros((tok_count, heads_here, width), jnp.float32),
        jnp.zeros((prefix_rows, width), jnp.float32),
    )
    backward_block_keys = lax.all_gather(latents, "leaf", axis=0, tiled=True)

    def advance(state):
        usable, logits = scores(backward_block_keys)
        probs = jnp.where(usable, jnp.exp(logits - log_norm[..., None]), 0.0)
        grad_weights = jnp.einsum(
            "thc,kc->thk", grad_latent, backward_block_keys, preferred_element_type=jnp.float32
        )
        grad_scores = (probs * (grad_weights - delta[..., None])).astype(jnp.bfloat16)
        query_acc = jnp.einsum(
            "thk,kc->thc", grad_scores, backward_block_keys, preferred_element_type=jnp.float32
        )
        contrib = softmax_scale * jnp.einsum(
            "thk,thc->kc", grad_scores, query_latent, preferred_element_type=jnp.float32
        )
        contrib = contrib + jnp.einsum(
            "thk,thc->kc",
            probs.astype(jnp.bfloat16),
            grad_latent,
            preferred_element_type=jnp.float32,
        )
        return (query_acc, contrib)

    query_acc, latent_grad = advance(backward_start)
    query_grad = (softmax_scale * query_acc).astype(jnp.bfloat16)
    d_queries = jnp.einsum(
        "thc,hdc->thd", query_grad, key_up_matrix, preferred_element_type=jnp.float32
    ).astype(jnp.bfloat16)
    owned_rows = lax.psum_scatter(
        latent_grad.astype(jnp.bfloat16), "leaf", scatter_dimension=0, tiled=True
    )
    d_latents = lax.psum(owned_rows, "head").astype(jnp.float32)
    return (d_queries, d_latents)


def solution(mesh):
    placed = (
        P("leaf", None),
        P("leaf", "head", None),
        P("leaf", "head", None),
        P("head", None, None),
        P("head", None, None),
        P(),
        P("leaf", None),
        P("leaf", None),
    )
    return jax.shard_map(
        on_device,
        mesh=mesh,
        in_specs=placed,
        out_specs=(P("leaf", "head", None), P("leaf", None)),
        check_vma=False,
    )
```

profile of v0, /device:TPU:2, one launch (start us, length us, event | category | flops | bytes accessed | tf_op | source)
XLA Modules:
  0.0 320.4 jit_solution(14642406166411518721)
XLA Ops:
  7.2 0.0 copy-start
  7.2 0.0 copy-start.1
  7.2 0.0 all-gather.2.cloned.1.call-start
  7.2 0.7 all-gather.2.cloned.1.call-update
  7.9 0.0 reduce-scatter.2.cloned.1.call-start
  8.0 0.8 reduce-window.8
  8.8 0.1 convert_reduce_fusion
  8.9 0.7 select_reduce_fusion
  9.6 1.0 convolution_minimum_fusion.8
  10.7 0.4 convolution_minimum_fusion.7
  11.1 0.4 convolution_minimum_fusion.6
  11.4 0.4 convolution_minimum_fusion.5
  11.8 0.4 convolution_minimum_fusion.4
  12.2 0.4 convolution_minimum_fusion.3
  12.6 0.4 convolution_minimum_fusion.2
  13.0 0.4 convolution_minimum_fusion.1
  13.4 0.4 convolution_minimum_fusion
  13.8 0.3 convolution_compare_fusion
  14.0 0.1 copy.34
  14.2 0.1 broadcast_bitcast_fusion
  14.3 0.4 copy.35
  14.7 0.0 copy-done
  14.7 1.5 fusion.23
  16.2 0.0 copy-done.1
  16.2 2.4 fusion.24
  18.6 0.0 copy-start.2
  18.6 74.2 %all-gather.2.cloned.1.call-done = bf16[2048,512]{1,0:T(8,128)(2,1)} async-done(((bf16[64,512]{1,0:T(8,128)(2,1)}), bf16[2048,512]{1,0:T(8,128)(2,1)}) %all-gather.2.cloned.1.call-update) | async-done | bytes 2097168 | tf_op jit(solution)/shard_map/all_gather | solution.py:93
  92.8 4.5 %fusion.3 = (f32[128,8]{0,1:T(8,128)S(1)}, f32[128,8,2048]{2,0,1:T(8,128)S(1)}) fusion(pred[128,2048]{1,0:T(8,128)(4,1)S(1)} %copy.35, bf16[128,8,512]{0,2,1:T(8,128)(2,1)S(1)} %fusion.23, bf16[2048,512]{1,0:T(8,128)(2,1)} %all-gather.2.cloned.1.call-done), kind=kOutput, calls=%fused_computation.7 | convolution fusion | flops 2153774080 | bytes 11800576 | tf_op jit(solution)/shard_map/thc,kc->thk/dot_general | solution.py:60
  97.3 2.7 fusion.1
  100.0 0.0 copy-done.2
  100.0 0.0 copy-start.3
  100.0 3.2 %fusion.4 = f32[2048,512,1]{1,0,2:T(8,128)S(1)} fusion(bf16[128,8,512]{0,2,1:T(8,128)(2,1)S(1)} %copy-done.2, f32[128,8,2048]{2,0,1:T(8,128)S(1)} %get-tuple-element.9, f32[128,8]{0,1:T(8,128)S(1)} %log_add_fusion, pred[128,2048]{1,0:T(8,128)(4,1)S(1)} %copy.35), kind=kOutput, calls=%fused_computation.8 | convolution fusion | flops 2157969408 | bytes 13897728 | tf_op jit(solution)/shard_map/thk,thc->kc/dot_general | solution.py:108
  103.3 0.0 copy-done.3
  103.3 2.8 multiply_reduce_fusion
  106.1 5.5 %multiply_convert_fusion = bf16[128,8,2048]{2,0,1:T(8,128)(2,1)S(1)} fusion(f32[128,8,2048]{2,0,1:T(8,128)S(1)} %get-tuple-element.9, f32[128,8]{0,1:T(8,128)S(1)} %multiply_reduce_fusion, f32[128,8]{0,1:T(8,128)S(1)} %log_add_fusion, pred[128,2048]{1,0:T(8,128)(4,1)S(1)} %copy.35, bf16[128,8,512]{0,2,1:T(8,128)(2,1)S(1)} %copy-done.2, ...), kind=kOutput, calls=%fused_computation | convolution fusion | flops 2162163712 | bytes 15998976 | tf_op jit(solution)/shard_map/thc,kc->thk/dot_general | solution.py:98
  111.6 0.0 copy-start.4
  111.6 1.9 copy-done.4
  113.5 4.0 %fusion.6 = bf16[2048,512]{1,0:T(8,128)(2,1)} fusion(f32[2048,512,1]{1,0,2:T(8,128)S(1)} %fusion.4, bf16[128,8,2048]{2,0,1:T(8,128)(2,1)S(1)} %multiply_convert_fusion, bf16[128,8,512]{0,2,1:T(8,128)(2,1)S(1)} %fusion.23), kind=kOutput, calls=%fused_computation.10 | convolution fusion | flops 2150629376 | bytes 11534336 | tf_op jit(solution)/shard_map/thk,thc->kc/dot_general | solution.py:105
  117.6 0.0 reduce-scatter.2.cloned.1.call-update
  117.6 0.0 all-reduce.2.cloned.1.call-start
  117.6 116.0 %reduce-scatter.2.cloned.1.call-done = bf16[64,512]{1,0:T(8,128)(2,1)} async-done(((bf16[2048,512]{1,0:T(8,128)(2,1)}), bf16[64,512]{1,0:T(8,128)(2,1)}) %reduce-scatter.2.cloned.1.call-update) | async-done | bytes 65552 | tf_op jit(solution)/shard_map/reduce_scatter | solution.py:121
  233.6 0.0 all-reduce.2.cloned.1.call-update
  233.7 5.5 %fusion.31 = bf16[128,8,128]{2,0,1:T(8,128)(2,1)S(1)} fusion(bf16[8,128,512]{2,1,0:T(8,128)(2,1)S(1)} %copy-done, bf16[128,8,2048]{2,0,1:T(8,128)(2,1)} %copy-done.4, bf16[2048,512]{1,0:T(8,128)(2,1)} %all-gather.2.cloned.1.call-done), kind=kOutput, calls=%fused_computation.42 | convolution fusion | flops 2282881024 | bytes 7602176 | tf_op jit(solution)/shard_map/thc,hdc->thd/dot_general | solution.py:118
  239.1 0.9 copy.46
  240.0 72.4 %all-reduce.2.cloned.1.call-done = bf16[64,512]{1,0:T(8,128)(2,1)} async-done(((bf16[64,512]{1,0:T(8,128)(2,1)}), bf16[64,512]{1,0:T(8,128)(2,1)}) %all-reduce.2.cloned.1.call-update) | async-done | bytes 65552 | tf_op jit(solution)/shard_map/psum | solution.py:124
  312.4 1.5 convert_element_type.57
  (2 shorter events, 0.0 us)
Async XLA Ops:
  7.2 7.6 %copy-start = (bf16[8,128,512]{2,1,0:T(8,128)(2,1)S(1)}, bf16[8,128,512]{2,1,0:T(8,128)(2,1)}, u32[]{:S(2)}) copy-start(bf16[8,128,512]{2,1,0:T(8,128)(2,1)} %param.11) | copy-start | bytes 3145732
  7.2 9.0 %copy-start.1 = (bf16[8,512,128]{2,1,0:T(8,128)(2,1)S(1)}, bf16[8,512,128]{2,1,0:T(8,128)(2,1)}, u32[]{:S(2)}) copy-start(bf16[8,512,128]{2,1,0:T(8,128)(2,1)} %param.12) | copy-start | bytes 3145732
  7.2 85.6 %all-gather.2.cloned.1.call-start = ((), (), s32[]{:S(2)}) async-start(), calls=%async_computation.1 | async-start | bytes 2162688 | tf_op jit(solution)/shard_map/all_gather | solution.py:93
  7.9 225.7 %reduce-scatter.2.cloned.1.call-start = ((), (), s32[]{:S(2)}) async-start(), calls=%async_computation.2 | async-start | bytes 2162688 | tf_op jit(solution)/shard_map/reduce_scatter | solution.py:121
  18.6 81.4 %copy-start.2 = (bf16[128,8,512]{0,2,1:T(8,128)(2,1)S(1)}, bf16[128,8,512]{0,2,1:T(8,128)(2,1)}, u32[]{:S(2)}) copy-start(bf16[128,8,512]{0,2,1:T(8,128)(2,1)} %fusion.24) | copy-start | bytes 3145732
  100.0 3.3 %copy-start.3 = (bf16[2048,512]{1,0:T(8,128)(2,1)S(1)}, bf16[2048,512]{1,0:T(8,128)(2,1)}, u32[]{:S(2)}) copy-start(bf16[2048,512]{1,0:T(8,128)(2,1)} %all-gather.2.cloned.1.call-done) | copy-start | bytes 6291460
  111.6 1.9 copy-start.4
  117.6 194.8 %all-reduce.2.cloned.1.call-start = ((), (), s32[]{:S(2)}) async-start(), calls=%async_computation.3 | async-start | bytes 131072 | tf_op jit(solution)/shard_map/psum | solution.py:124
Sparse Core Ops, SparseCore 0:
  10.8 81.9 all-gather.1
  117.7 115.8 reduce-scatter.1
  236.4 75.8 all-reduce.1
where the time goes:
time: 321 us; the launch traced here: 320 us
  waiting for transfers between devices  263 us (82%)
  matrix products  33.7 us (10%)
  between operations  14 us (4%)
  other arithmetic  5.85 us (2%)
  local copies, waits for them, and re-layouts  3.47 us (1%)
    reduce_scatter x1, waiting for transfers between devices, on_device(): lax.psum_scatter(latent_grad.astype(jnp.bfloat16), 'leaf', scatter_dimens...  116 us
    all_gather x1, waiting for transfers between devices, on_device(): backward_block_keys = lax.all_gather(latents, 'leaf', axis=0, tiled=True)  74.2 us
    psum x1, waiting for transfers between devices, on_device(): d_latents = lax.psum(owned_rows, 'head').astype(jnp.float32)  72.4 us
  transfers between devices with their start and end apart: 3, of which 3 were waited for; matrix products, arithmetic and copies ran while one was open for 5% of the time, Pallas kernels for 0%

commit v1 on v0

v1 whole, which is shorter than its diff:
```python
import jax
import jax.numpy as jnp
from jax import lax
from jax.experimental import pallas as pl
from jax.experimental.pallas import tpu as pltpu
from jax.sharding import PartitionSpec as P

MESH = pl.DeviceIdType.MESH
NODE_LEN = 8
SCALE = 192.0 ** (-0.5)
LOG2E = 1.4426950408889634
MASKED = -1e30
LAG = 3
F32 = jnp.float32
BF16 = jnp.bfloat16


def dot(a, b):
    return jnp.dot(a, b, preferred_element_type=F32)


def place():
    leaf = lax.axis_index("leaf")
    head = lax.axis_index("head")
    x = (leaf // 16) * 2 + head // 4
    return x, lax.rem(head, 4), lax.rem(leaf // 2, 8), lax.rem(leaf, 2)


def device(x, y, z, c):
    return ((x // 2) * 16 + z * 2 + c, lax.rem(x, 2) * 4 + y)


def step_offset(s):
    half = (s + 1) // 2
    return 4 + jnp.where(lax.rem(s, 2) == 1, -half, half)


def kernel(
    lat_ref, par_ref, node_ref, len_ref, q_hbm, g_hbm, ku_hbm, vu_hbm,
    dq_ref, dl_ref,
    q_in, g_in, ku, vu, wide, keys, keys_t, ql, gl, ql_t, gl_t, live_t,
    w_buf, gw_buf, gs_buf, m_grp, m_run, l_run, d_run,
    cont, core_out, core_in, axis_out, axis_in, z_out, z_in, z_own,
    sum_a, sum_b, last_a, last_b, out_a, out_b,
    in_sem, ag_send, x_recv, z_recv, c_recv,
    core_send, core_recv, ax_send, ax_recv, zs_send, zs_recv,
    t1_send, t1_recv, t2_send, t2_recv,
):
    x, y, z, c = place()
    x_hi = x // 2
    at = lambda dx, dy, dz: device(
        lax.rem(x + dx + 4, 4), lax.rem(y + dy + 4, 4), lax.rem(z + dz + 8, 8), c
    )
    sibling = device(x, y, z, 1 - c)
    partner = device(3 - x, y, z, c)

    loads = [
        pltpu.make_async_copy(src, dst, in_sem.at[i])
        for i, (src, dst) in enumerate(((q_hbm, q_in), (ku_hbm, ku), (g_hbm, g_in), (vu_hbm, vu)))
    ]
    for load in loads:
        load.start()

    barrier = pltpu.get_barrier_semaphore()
    peers = [sibling, at(0, 0, 1), at(0, 0, -1)]
    peers += [at(k, 0, 0) for k in (1, 2, 3)] + [at(0, k, 0) for k in (1, 2, 3)]
    for peer in peers:
        pl.semaphore_signal(barrier, inc=1, device_id=peer, device_id_type=MESH)
    keys[z, c, x_hi] = lat_ref[...]
    pl.semaphore_wait(barrier, len(peers))

    sent = []

    def send(block, recv_sem, peer):
        copy = pltpu.make_async_remote_copy(
            src_ref=block, dst_ref=block, send_sem=ag_send.at[len(sent)], recv_sem=recv_sem,
            device_id=peer, device_id_type=MESH,
        )
        copy.start()
        sent.append(copy)

    def arrived(block, recv_sem):
        pltpu.make_async_remote_copy(
            src_ref=block, dst_ref=block, send_sem=ag_send.at[0], recv_sem=recv_sem,
            device_id=sibling, device_id_type=MESH,
        ).wait_recv()

    mine = (x_hi, 1 - x_hi)
    own = keys.at[z, c, x_hi]
    send(own, x_recv.at[0], partner)
    send(own, z_recv.at[0, 0, 0], at(0, 0, 1))
    send(own, z_recv.at[1, 0, 0], at(0, 0, -1))
    send(own, c_recv.at[0, 0], sibling)

    def latents_of(src_ref, mat, out_ref, out_t_ref, turned):
        wide[...] = src_ref[...].astype(F32).reshape(wide.shape)
        for h in range(8):
            rows = wide[pl.ds(h, 128, stride=8), :].astype(BF16)
            if turned:
                val = lax.dot_general(
                    rows, mat[h], (((1,), (1,)), ((), ())), preferred_element_type=F32
                )
            else:
                val = dot(rows, mat[h])
            low = val.astype(BF16)
            out_ref[h * 128 : (h + 1) * 128, :] = low
            out_t_ref[:, h * 128 : (h + 1) * 128] = low.T

    loads[0].wait()
    loads[1].wait()
    latents_of(q_in, ku, ql, ql_t, False)

    other = keys.at[z, c, 1 - x_hi]
    arrived(other, x_recv.at[0])
    send(other, z_recv.at[0, 0, 1], at(0, 0, 1))
    send(other, z_recv.at[1, 0, 1], at(0, 0, -1))
    send(other, c_recv.at[0, 1], sibling)

    loads[2].wait()
    loads[3].wait()
    latents_of(g_in, vu, gl, gl_t, True)

    def forward(dist):
        for way in (0, 1):
            for kind in (0, 1):
                if dist == 4 and way != kind:
                    continue
                sign = 1 if way == 0 else -1
                origin = lax.rem(z - sign * dist + 8, 8)
                block = keys.at[origin, c, mine[kind]]
                arrived(block, z_recv.at[way, dist - 1, kind])
                if dist < 3 or (dist == 3 and way == kind):
                    send(block, z_recv.at[way, dist, kind], at(0, 0, sign))
                slot = 2 * dist - 1 + (way if dist < 4 else 0)
                send(block, c_recv.at[slot, kind], sibling)

    forward(1)

    above = lax.broadcasted_iota(jnp.int32, (256, 256), 0)
    below = lax.broadcasted_iota(jnp.int32, (256, 256), 1)
    linked = (above == par_ref[...]) | (above == below)
    reach = jnp.where(linked, 1.0, 0.0).astype(BF16)
    for _ in range(8):
        reach = jnp.minimum(dot(reach, reach), 1.0).astype(BF16)
    spot = lax.broadcasted_iota(jnp.int32, (256, 128), 1)
    node = lax.broadcasted_iota(jnp.int32, (256, 128), 0)
    token_node = jnp.full((256, 128), node_ref[0, 0], jnp.int32)
    bound = len_ref[0, 0]
    for b in range(1, 8):
        token_node = jnp.where(spot >= bound, node_ref[0, b], token_node)
        bound = bound + len_ref[0, b]
    picked = jnp.where(token_node == node, 1.0, 0.0).astype(BF16)
    live_t[...] = dot(reach, picked).astype(BF16)

    m_run[...] = jnp.full(m_run.shape, MASKED, F32)
    l_run[...] = jnp.zeros(l_run.shape, F32)
    d_run[...] = jnp.zeros(d_run.shape, F32)

    def score_group(plane):
        group = keys[plane].reshape(256, 512)
        keys_t[:, pl.ds(pl.multiple_of(plane * 256, 256), 256)] = group.T
        row = lax.broadcasted_iota(jnp.int32, (256, 256), 0)
        col = lax.broadcasted_iota(jnp.int32, (256, 256), 1)
        half, which, inner = row // 128, lax.rem(row // 64, 2), lax.rem(row, 64) // NODE_LEN
        key_node = ((which * 8 + plane) * 2 + half) * NODE_LEN + inner
        spread = jnp.where(key_node == col, 1.0, 0.0).astype(BF16)
        bias = (dot(spread, live_t[...]) - 1.0) * (-MASKED)
        bias = jnp.concatenate([bias, bias], axis=1)
        for tile in range(4):
            cols = slice(tile * 256, (tile + 1) * 256)
            s = dot(group, ql_t[:, cols]) * (SCALE * LOG2E) + bias
            gw = dot(group, gl_t[:, cols])
            m_old = m_run[:, cols]
            m_new = jnp.maximum(m_old, jnp.max(s, axis=0, keepdims=True))
            w = jnp.exp2(s - m_new)
            alpha = jnp.exp2(m_old - m_new)
            l_run[:, cols] = alpha * l_run[:, cols] + jnp.sum(w, axis=0, keepdims=True)
            low = w.astype(BF16).astype(F32)
            d_run[:, cols] = alpha * d_run[:, cols] + jnp.sum(low * gw, axis=0, keepdims=True)
            m_run[:, cols] = m_new
            m_grp[plane, :, cols] = m_new
            w_buf[plane, :, cols] = w
            gw_buf[plane, :, cols] = gw

    def sibling_blocks(origin, slot):
        for kind in (0, 1):
            arrived(keys.at[origin, 1 - c, mine[kind]], c_recv.at[slot, kind])

    def scores(slots):
        first, count = slots

        def body(i, _):
            slot = first + i
            dist = (slot + 1) // 2
            sign = jnp.where(lax.rem(slot, 2) == 1, -1, 1)
            score_group(lax.rem(z + sign * dist + 8, 8))
            return 0

        lax.fori_loop(0, count, body, 0)

    sibling_blocks(z, 0)
    scores((0, 1))
    for dist in (1, 2, 3):
        forward(dist + 1)
        sibling_blocks(lax.rem(z - dist + 8, 8), 2 * dist - 1)
        sibling_blocks(lax.rem(z + dist, 8), 2 * dist)
        scores((2 * dist - 1, 2))
    sibling_blocks(lax.rem(z + 4, 8), 7)
    scores((7, 1))

    inv = 1.0 / l_run[...]
    l_run[...] = inv
    d_run[...] = d_run[...] * inv

    def core_copy(s):
        return pltpu.make_async_remote_copy(
            src_ref=core_out.at[s], dst_ref=core_in.at[s], send_sem=core_send.at[s],
            recv_sem=core_recv.at[s], device_id=sibling, device_id_type=MESH,
        )

    def axis_copies(s):
        copies = []
        for part in (0, 1):
            for k in (1, 2, 3):
                place_of = lax.rem((x if part == 0 else y) + k, 4)
                copies.append(
                    pltpu.make_async_remote_copy(
                        src_ref=axis_out.at[s, part, place_of], dst_ref=axis_in.at[s, part, k - 1],
                        send_sem=ax_send.at[s, part, k - 1], recv_sem=ax_recv.at[s, part, k - 1],
                        device_id=at(k, 0, 0) if part == 0 else at(0, k, 0), device_id_type=MESH,
                    )
                )
        return copies

    def z_copy(s):
        return pltpu.make_async_remote_copy(
            src_ref=z_out.at[s], dst_ref=z_in.at[s], send_sem=zs_send.at[s],
            recv_sem=zs_recv.at[s], device_id=at(0, 0, step_offset(s)), device_id_type=MESH,
        )

    def contribution(s):
        plane = lax.rem(z + step_offset(s), 8)
        total = None
        for tile in range(4):
            cols = slice(tile * 256, (tile + 1) * 256)
            factor = jnp.exp2(m_grp[plane, :, cols] - m_run[:, cols]) * l_run[:, cols]
            p = w_buf[plane, :, cols] * factor
            gs = (p * (gw_buf[plane, :, cols] - d_run[:, cols])).astype(BF16)
            gs_buf[pl.ds(pl.multiple_of(plane * 256, 256), 256), cols] = gs
            term = dot(gs, ql[cols, :]) * SCALE + dot(p.astype(BF16), gl[cols, :])
            total = term if total is None else total + term
        slot = lax.rem(s, 2)
        cont[slot] = total.reshape(2, 2, 64, 512)
        for part in (0, 1):
            for j in range(4):
                core_out[s, part, j] = cont[
                    slot, 1 - c, :, part * 32 : (part + 1) * 32, j * 128 : (j + 1) * 128
                ].astype(BF16)
        core_copy(s).start()

    def core_sum(s):
        core_copy(s).wait()
        slot = lax.rem(s, 2)
        for part in (0, 1):
            for j in range(4):
                axis_out[s, part, j] = (
                    cont[slot, c, :, part * 32 : (part + 1) * 32, j * 128 : (j + 1) * 128]
                    + core_in[s, part, j].astype(F32)
                ).astype(BF16)
        for copy in axis_copies(s):
            copy.start()

    def axis_sum(s, last):
        for copy in axis_copies(s):
            copy.wait()
        for part in (0, 1):
            total = axis_out[s, part, x if part == 0 else y].astype(F32)
            for k in range(3):
                total = total + axis_in[s, part, k].astype(F32)
            if last:
                z_own[part] = total
            else:
                z_out[s, part] = total.astype(BF16)
        if not last:
            z_copy(s).start()

    def reduce_step(s, _):
        contribution(s)

        @pl.when(s >= 1)
        def _():
            core_sum(s - 1)

        @pl.when(s >= 1 + LAG)
        def _():
            axis_sum(s - 1 - LAG, False)

        return 0

    lax.fori_loop(0, 8, reduce_step, 0)

    def query_tile(tile):
        cols = slice(tile * 256, (tile + 1) * 256)
        grad = (dot(keys_t[...], gs_buf[:, cols]) * SCALE).astype(BF16)
        for i in (0, 1):
            h = 2 * tile + i
            out = dot(ku[h], grad[:, i * 128 : (i + 1) * 128])
            wide[pl.ds(h, 128, stride=8), :] = out.T

    core_sum(7)
    query_tile(0)
    for s in range(7 - LAG, 7):
        axis_sum(s, False)
    query_tile(1)
    axis_sum(7, True)
    for s in range(7):
        z_copy(s).wait()
    for part in (0, 1):
        total = z_own[part]
        for s in range(7):
            total = total + z_in[s, part].astype(F32)
        if part == 0:
            sum_a[y] = total.astype(BF16)
        else:
            out_b[...] = total.astype(BF16)
            sum_b[x] = out_b[x_hi]

    first = []
    for k in (1, 2, 3):
        first.append(
            pltpu.make_async_remote_copy(
                src_ref=sum_a.at[y], dst_ref=sum_a.at[y], send_sem=t1_send.at[0, k - 1],
                recv_sem=t1_recv.at[0, k - 1], device_id=at(0, k, 0), device_id_type=MESH,
            )
        )
        their_hi = lax.rem(x + k, 4) // 2
        first.append(
            pltpu.make_async_remote_copy(
                src_ref=out_b.at[their_hi], dst_ref=sum_b.at[x], send_sem=t1_send.at[1, k - 1],
                recv_sem=t1_recv.at[1, k - 1], device_id=at(k, 0, 0), device_id_type=MESH,
            )
        )
    for copy in first:
        copy.start()
    query_tile(2)
    query_tile(3)
    dq_ref[...] = wide[...].reshape(128, 8, 128).astype(BF16)
    for copy in first:
        copy.wait()

    out_a[...] = (
        sum_a[0].astype(F32) + sum_a[1].astype(F32) + sum_a[2].astype(F32) + sum_a[3].astype(F32)
    ).astype(BF16)
    last_a[x] = out_a[x_hi]
    last_b[y] = (
        sum_b[0].astype(F32) + sum_b[1].astype(F32) + sum_b[2].astype(F32) + sum_b[3].astype(F32)
    ).astype(BF16)
    second = []
    for k in (1, 2, 3):
        their_hi = lax.rem(x + k, 4) // 2
        second.append(
            pltpu.make_async_remote_copy(
                src_ref=out_a.at[their_hi], dst_ref=last_a.at[x], send_sem=t2_send.at[0, k - 1],
                recv_sem=t2_recv.at[0, k - 1], device_id=at(k, 0, 0), device_id_type=MESH,
            )
        )
        second.append(
            pltpu.make_async_remote_copy(
                src_ref=last_b.at[y], dst_ref=last_b.at[y], send_sem=t2_send.at[1, k - 1],
                recv_sem=t2_recv.at[1, k - 1], device_id=at(0, k, 0), device_id_type=MESH,
            )
        )
    for copy in second:
        copy.start()
    for copy in sent:
        copy.wait_send()
    for copy in second:
        copy.wait()
    for j in range(4):
        dl_ref[0:32, j * 128 : (j + 1) * 128] = last_a[j].astype(F32)
        dl_ref[32:64, j * 128 : (j + 1) * 128] = last_b[j].astype(F32)


def on_device(
    latents, queries, grad_out, key_up_matrix, value_up_matrix, parents, branch_node, branch_lengths
):
    vmem = pl.BlockSpec(memory_space=pltpu.VMEM)
    smem = pl.BlockSpec(memory_space=pltpu.SMEM)
    anywhere = pl.BlockSpec(memory_space=pl.ANY)
    dma = pltpu.SemaphoreType.DMA
    tile = (2, 32, 128)
    return pl.pallas_call(
        kernel,
        name="tree_attention_backward",
        out_shape=(
            jax.ShapeDtypeStruct((128, 8, 128), BF16),
            jax.ShapeDtypeStruct((64, 512), F32),
        ),
        in_specs=[vmem, vmem, smem, smem, anywhere, anywhere, anywhere, anywhere],
        out_specs=(vmem, vmem),
        scratch_shapes=[
            pltpu.VMEM((128, 8, 128), BF16),
            pltpu.VMEM((128, 8, 128), BF16),
            pltpu.VMEM((8, 128, 512), BF16),
            pltpu.VMEM((8, 512, 128), BF16),
            pltpu.VMEM((1024, 128), F32),
            pltpu.VMEM((8, 2, 2, 64, 512), BF16),
            pltpu.VMEM((512, 2048), BF16),
            pltpu.VMEM((1024, 512), BF16),
            pltpu.VMEM((1024, 512), BF16),
            pltpu.VMEM((512, 1024), BF16),
            pltpu.VMEM((512, 1024), BF16),
            pltpu.VMEM((256, 128), BF16),
            pltpu.VMEM((8, 256, 1024), F32),
            pltpu.VMEM((8, 256, 1024), F32),
            pltpu.VMEM((2048, 1024), BF16),
            pltpu.VMEM((8, 1, 1024), F32),
            pltpu.VMEM((1, 1024), F32),
            pltpu.VMEM((1, 1024), F32),
            pltpu.VMEM((1, 1024), F32),
            pltpu.VMEM((2, 2, 2, 64, 512), F32),
            pltpu.VMEM((8, 2, 4) + tile, BF16),
            pltpu.VMEM((8, 2, 4) + tile, BF16),
            pltpu.VMEM((8, 2, 4) + tile, BF16),
            pltpu.VMEM((8, 2, 3) + tile, BF16),
            pltpu.VMEM((7, 2) + tile, BF16),
            pltpu.VMEM((7, 2) + tile, BF16),
            pltpu.VMEM((2,) + tile, F32),
            pltpu.VMEM((4,) + tile, BF16),
            pltpu.VMEM((4, 32, 128), BF16),
            pltpu.VMEM((4, 32, 128), BF16),
            pltpu.VMEM((4, 32, 128), BF16),
            pltpu.VMEM(tile, BF16),
            pltpu.VMEM(tile, BF16),
            dma((4,)),
            dma((35,)),
            dma((1,)),
            dma((2, 4, 2)),
            dma((8, 2)),
            dma((8,)),
            dma((8,)),
            dma((8, 2, 3)),
            dma((8, 2, 3)),
            dma((7,)),
            dma((7,)),
            dma((2, 3)),
            dma((2, 3)),
            dma((2, 3)),
            dma((2, 3)),
        ],
        compiler_params=pltpu.CompilerParams(
            collective_id=0, has_side_effects=True, vmem_limit_bytes=58 * 1024 * 1024
        ),
    )(
        latents, parents.reshape(1, 256), branch_node, branch_lengths,
        queries, grad_out, key_up_matrix, value_up_matrix,
    )


def solution(mesh):
    placed = (
        P("leaf", None),
        P("leaf", "head", None),
        P("leaf", "head", None),
        P("head", None, None),
        P("head", None, None),
        P(),
        P("leaf", None),
        P("leaf", None),
    )
    return jax.shard_map(
        on_device,
        mesh=mesh,
        in_specs=placed,
        out_specs=(P("leaf", "head", None), P("leaf", None)),
        check_vma=False,
    )
```

time: 321 us -> 60.2 us (0.19)
  waiting for transfers between devices: 263 us -> 0 us
  Pallas kernels: 0 us -> 56.8 us
  matrix products: 33.7 us -> 0 us
  between operations: 14 us -> 0.65 us
  other arithmetic: 5.85 us -> 0 us
    reduce_scatter x1 -> x0, waiting for transfers between devices: 116 us -> none  [on_device(): lax.psum_scatter(latent_grad.astype(jnp.bfloat16), 'leaf', scatter_dimens...]
    all_gather x1 -> x0, waiting for transfers between devices: 74.2 us -> none  [on_device(): backward_block_keys = lax.all_gather(latents, 'leaf', axis=0, tiled=True)]
    psum x1 -> x0, waiting for transfers between devices: 72.4 us -> none  [on_device(): d_latents = lax.psum(owned_rows, 'head').astype(jnp.float32)]
    pallas_call x0 -> x1, Pallas kernels: none -> 56.8 us  [on_device(): pl.pallas_call(kernel, name='tree_attention_backward', out_shape=(jax.Sha...]
    dot_general x18 -> x0, matrix products: 33.7 us -> none  [the longest x1 5.47 us: advance(): jnp.einsum('thc,kc->thk', grad_latent, backward_block_keys, preferred_ele...]
    reduce_sum x3 -> x0, other arithmetic: 3.51 us -> none  [the longest x1 2.68 us: advance(): return (new_max, jnp.sum(weights, axis=-1), weighted)]
  transfers between devices with their start and end apart: 3 -> 0, of which waited for: 3 -> 0; matrix products, arithmetic and copies ran while one was open for 5% -> 0% of each run, Pallas kernels for 0% -> 0%
where the time goes in v1:
time: 60.2 us; the launch traced here: 59.8 us
  Pallas kernels  56.8 us (94%)
  local copies, waits for them, and re-layouts  2.36 us (4%)
  between operations  0.65 us (1%)
    pallas_call x1, Pallas kernels, on_device(): pl.pallas_call(kernel, name='tree_attention_backward', out_shape=(jax.Sha...  56.8 us
    unnamed x4, local copies, waits for them, and re-layouts  2.36 us

profile of v1, /device:TPU:2, one launch (start us, length us, event | category | flops | bytes accessed | tf_op | source)
XLA Modules:
  0.0 59.8 jit_solution(4840653668399889554)
XLA Ops:
  0.6 56.8 %tree_attention_backward.1 = (bf16[128,8,128]{2,1,0:T(8,128)(2,1)}, f32[64,512]{1,0:T(8,128)}) custom-call(bf16[64,512]{1,0:T(8,128)(2,1)} %lat_ref.1, s32[1,256]{1,0:T(1,128)} %bitcast.1, s32[1,8]{1,0:T(1,128)} %node_ref.1, s32[1,8]{1,0:T(1,128)} %len_ref.1, bf16[128,8,128]{2,1,0:T(8,128)(2,1)} %q_hbm.1, bf16[128,8,128]{2,1,0:T(8,128)(2,1)} %g_hbm.1, ...), custom_call_target="tpu_custom_call" | custom-call | tf_op jit(solution)/shard_map/tree_attention_backward/pallas_call | solution.py:392
  57.4 0.0 copy-start
  57.4 1.7 %copy.12 = bf16[128,8,128]{2,1,0:T(8,128)(2,1)} copy(bf16[128,8,128]{2,1,0:T(8,128)(2,1)} %get-tuple-element.4) | data formatting | bytes 524288
  59.1 0.0 copy-done
  59.1 0.7 %copy.13 = f32[64,512]{1,0:T(8,128)} copy(f32[64,512]{1,0:T(8,128)S(1)} %copy-done) | data formatting | bytes 262144
Async XLA Ops:
  57.4 1.7 %copy-start = (f32[64,512]{1,0:T(8,128)S(1)}, f32[64,512]{1,0:T(8,128)}, u32[]{:S(2)}) copy-start(f32[64,512]{1,0:T(8,128)} %get-tuple-element.5) | copy-start | bytes 393220

commit v2 on v1

--- a/solution.py
+++ b/solution.py
@@ -10,7 +10,6 @@
 SCALE = 192.0 ** (-0.5)
 LOG2E = 1.4426950408889634
 MASKED = -1e30
-LAG = 3
 F32 = jnp.float32
 BF16 = jnp.bfloat16
 
@@ -31,8 +30,7 @@
 
 
 def step_offset(s):
-    half = (s + 1) // 2
-    return 4 + jnp.where(lax.rem(s, 2) == 1, -half, half)
+    return (4, 3, 5, 2, 6, 1, 7, 0)[s]
 
 
 def kernel(
@@ -42,7 +40,7 @@
     w_buf, gw_buf, gs_buf, m_grp, m_run, l_run, d_run,
     cont, core_out, core_in, axis_out, axis_in, z_out, z_in, z_own,
     sum_a, sum_b, last_a, last_b, out_a, out_b,
-    in_sem, ag_send, x_recv, z_recv, c_recv,
+    in_sem, ag_send, x_recv, z_recv, n_recv, c_recv,
     core_send, core_recv, ax_send, ax_recv, zs_send, zs_recv,
     t1_send, t1_recv, t2_send, t2_recv,
 ):
@@ -62,11 +60,11 @@
         load.start()
 
     barrier = pltpu.get_barrier_semaphore()
-    peers = [sibling, at(0, 0, 1), at(0, 0, -1)]
+    peers = [sibling] + [at(0, 0, k) for k in range(1, 8)]
     peers += [at(k, 0, 0) for k in (1, 2, 3)] + [at(0, k, 0) for k in (1, 2, 3)]
     for peer in peers:
         pl.semaphore_signal(barrier, inc=1, device_id=peer, device_id_type=MESH)
-    keys[z, c, x_hi] = lat_ref[...]
+    keys[z, c, x_hi] = lat_ref[...].reshape(4, 16, 512)
     pl.semaphore_wait(barrier, len(peers))
 
     sent = []
@@ -85,12 +83,22 @@
             device_id=sibling, device_id_type=MESH,
         ).wait_recv()
 
-    mine = (x_hi, 1 - x_hi)
-    own = keys.at[z, c, x_hi]
-    send(own, x_recv.at[0], partner)
-    send(own, z_recv.at[0, 0, 0], at(0, 0, 1))
-    send(own, z_recv.at[1, 0, 0], at(0, 0, -1))
-    send(own, c_recv.at[0, 0], sibling)
+    colour = lambda x, y: lax.rem(y + 2 * lax.rem(x, 2), 4)
+    flip = device(x + 1 - 2 * lax.rem(x, 2), y, z, c)
+    neighbours = (at(0, 1, 0), at(0, -1, 0), flip)
+    mine = colour(x, y)
+    theirs = (lax.rem(mine + 3, 4), lax.rem(mine + 1, 4), lax.rem(mine + 2, 4))
+    kinds = (x_hi, 1 - x_hi)
+    far_first = (4, 3, 5, 2, 6, 1, 7)
+    near_first = (1, 7, 2, 6, 3, 5, 4)
+
+    def spread_z(kind):
+        for k in far_first:
+            send(keys.at[z, c, kinds[kind], mine], z_recv.at[k - 1, kind], at(0, 0, k))
+
+    send(keys.at[z, c, x_hi], x_recv.at[0], partner)
+    spread_z(0)
+    send(keys.at[z, c, x_hi], c_recv.at[7, 0], sibling)
 
     def latents_of(src_ref, mat, out_ref, out_t_ref, turned):
         wide[...] = src_ref[...].astype(F32).reshape(wide.shape)
@@ -110,31 +118,20 @@
     loads[1].wait()
     latents_of(q_in, ku, ql, ql_t, False)
 
-    other = keys.at[z, c, 1 - x_hi]
-    arrived(other, x_recv.at[0])
-    send(other, z_recv.at[0, 0, 1], at(0, 0, 1))
-    send(other, z_recv.at[1, 0, 1], at(0, 0, -1))
-    send(other, c_recv.at[0, 1], sibling)
+    arrived(keys.at[z, c, 1 - x_hi], x_recv.at[0])
+    spread_z(1)
+    send(keys.at[z, c, 1 - x_hi], c_recv.at[7, 1], sibling)
 
     loads[2].wait()
     loads[3].wait()
     latents_of(g_in, vu, gl, gl_t, True)
 
-    def forward(dist):
-        for way in (0, 1):
-            for kind in (0, 1):
-                if dist == 4 and way != kind:
-                    continue
-                sign = 1 if way == 0 else -1
-                origin = lax.rem(z - sign * dist + 8, 8)
-                block = keys.at[origin, c, mine[kind]]
-                arrived(block, z_recv.at[way, dist - 1, kind])
-                if dist < 3 or (dist == 3 and way == kind):
-                    send(block, z_recv.at[way, dist, kind], at(0, 0, sign))
-                slot = 2 * dist - 1 + (way if dist < 4 else 0)
-                send(block, c_recv.at[slot, kind], sibling)
-
-    forward(1)
+    def spread_replicas(kind):
+        for k in near_first:
+            piece = keys.at[lax.rem(z - k + 8, 8), c, kinds[kind], mine]
+            arrived(piece, z_recv.at[k - 1, kind])
+            for i in range(3):
+                send(piece, n_recv.at[k - 1, kind, i], neighbours[i])
 
     above = lax.broadcasted_iota(jnp.int32, (256, 256), 0)
     below = lax.broadcasted_iota(jnp.int32, (256, 256), 1)
@@ -156,16 +153,22 @@
     l_run[...] = jnp.zeros(l_run.shape, F32)
     d_run[...] = jnp.zeros(d_run.shape, F32)
 
-    def score_group(plane):
-        group = keys[plane].reshape(256, 512)
-        keys_t[:, pl.ds(pl.multiple_of(plane * 256, 256), 256)] = group.T
-        row = lax.broadcasted_iota(jnp.int32, (256, 256), 0)
-        col = lax.broadcasted_iota(jnp.int32, (256, 256), 1)
-        half, which, inner = row // 128, lax.rem(row // 64, 2), lax.rem(row, 64) // NODE_LEN
-        key_node = ((which * 8 + plane) * 2 + half) * NODE_LEN + inner
+    spread_replicas(0)
+
+    def score_blocks(kind, planes):
+        which = kinds[kind]
+        rows = 128 * len(planes)
+        row = lax.broadcasted_iota(jnp.int32, (rows, 256), 0)
+        col = lax.broadcasted_iota(jnp.int32, (rows, 256), 1)
+        plane_of = jnp.zeros((rows, 256), jnp.int32)
+        for n, plane in enumerate(planes):
+            plane_of = jnp.where(row // 128 == n, plane, plane_of)
+        half, inner = lax.rem(row // 64, 2), lax.rem(row, 64) // NODE_LEN
+        key_node = ((which * 8 + plane_of) * 2 + half) * NODE_LEN + inner
         spread = jnp.where(key_node == col, 1.0, 0.0).astype(BF16)
         bias = (dot(spread, live_t[...]) - 1.0) * (-MASKED)
         bias = jnp.concatenate([bias, bias], axis=1)
+        group = jnp.concatenate([keys[plane, :, which].reshape(128, 512) for plane in planes], axis=0)
         for tile in range(4):
             cols = slice(tile * 256, (tile + 1) * 256)
             s = dot(group, ql_t[:, cols]) * (SCALE * LOG2E) + bias
@@ -178,35 +181,40 @@
             low = w.astype(BF16).astype(F32)
             d_run[:, cols] = alpha * d_run[:, cols] + jnp.sum(low * gw, axis=0, keepdims=True)
             m_run[:, cols] = m_new
-            m_grp[plane, :, cols] = m_new
-            w_buf[plane, :, cols] = w
-            gw_buf[plane, :, cols] = gw
-
-    def sibling_blocks(origin, slot):
-        for kind in (0, 1):
-            arrived(keys.at[origin, 1 - c, mine[kind]], c_recv.at[slot, kind])
-
-    def scores(slots):
-        first, count = slots
-
-        def body(i, _):
-            slot = first + i
-            dist = (slot + 1) // 2
-            sign = jnp.where(lax.rem(slot, 2) == 1, -1, 1)
-            score_group(lax.rem(z + sign * dist + 8, 8))
-            return 0
-
-        lax.fori_loop(0, count, body, 0)
-
-    sibling_blocks(z, 0)
-    scores((0, 1))
-    for dist in (1, 2, 3):
-        forward(dist + 1)
-        sibling_blocks(lax.rem(z - dist + 8, 8), 2 * dist - 1)
-        sibling_blocks(lax.rem(z + dist, 8), 2 * dist)
-        scores((2 * dist - 1, 2))
-    sibling_blocks(lax.rem(z + 4, 8), 7)
-    scores((7, 1))
+            for n, plane in enumerate(planes):
+                part = slice(n * 128, (n + 1) * 128)
+                m_grp[plane, which, :, cols] = m_new
+                w_buf[plane, :, which, :, cols] = w[part].reshape(2, 64, 256)
+                gw_buf[plane, :, which, :, cols] = gw[part].reshape(2, 64, 256)
+
+    def complete(kind, steps):
+        for k in steps:
+            block = keys.at[lax.rem(z - k + 8, 8), c, kinds[kind]]
+            for i in range(3):
+                piece = keys.at[lax.rem(z - k + 8, 8), c, kinds[kind], theirs[i]]
+                arrived(piece, n_recv.at[k - 1, kind, i])
+            send(block, c_recv.at[k - 1, kind], sibling)
+
+    def score_from(kind, steps):
+        planes = []
+        for k in steps:
+            plane = lax.rem(z - k + 8, 8)
+            arrived(keys.at[plane, 1 - c, kinds[kind]], c_recv.at[(k - 1) % 8, kind])
+            if kind == 1:
+                keys_t[:, pl.ds(pl.multiple_of(plane * 256, 256), 256)] = (
+                    keys[plane].reshape(256, 512).T
+                )
+            planes.append(plane)
+        score_blocks(kind, planes)
+
+    spread_replicas(1)
+    complete(0, near_first)
+    score_from(0, (0,) + near_first[:3])
+    complete(1, near_first[:3])
+    score_from(0, near_first[3:])
+    complete(1, near_first[3:])
+    score_from(1, (0,) + near_first[:3])
+    score_from(1, near_first[3:])
 
     inv = 1.0 / l_run[...]
     l_run[...] = inv
@@ -238,29 +246,42 @@
             recv_sem=zs_recv.at[s], device_id=at(0, 0, step_offset(s)), device_id_type=MESH,
         )
 
-    def contribution(s):
-        plane = lax.rem(z + step_offset(s), 8)
+    def contribution(*steps):
+        planes = [lax.rem(z + step_offset(s), 8) for s in steps]
         total = None
         for tile in range(4):
             cols = slice(tile * 256, (tile + 1) * 256)
-            factor = jnp.exp2(m_grp[plane, :, cols] - m_run[:, cols]) * l_run[:, cols]
-            p = w_buf[plane, :, cols] * factor
-            gs = (p * (gw_buf[plane, :, cols] - d_run[:, cols])).astype(BF16)
-            gs_buf[pl.ds(pl.multiple_of(plane * 256, 256), 256), cols] = gs
-            term = dot(gs, ql[cols, :]) * SCALE + dot(p.astype(BF16), gl[cols, :])
+            probs, grads = [], []
+            for plane in planes:
+                factor = [
+                    jnp.exp2(m_grp[plane, which, :, cols] - m_run[:, cols]) * l_run[:, cols]
+                    for which in (0, 1)
+                ]
+                for half in (0, 1):
+                    for which in (0, 1):
+                        p = w_buf[plane, half, which, :, cols] * factor[which]
+                        gw = gw_buf[plane, half, which, :, cols]
+                        grads.append((p * (gw - d_run[:, cols])).astype(BF16))
+                        probs.append(p.astype(BF16))
+                gs_buf[pl.ds(pl.multiple_of(plane * 256, 256), 256), cols] = jnp.concatenate(
+                    grads[-4:], axis=0
+                )
+            gs, p_low = jnp.concatenate(grads, axis=0), jnp.concatenate(probs, axis=0)
+            term = dot(gs, ql[cols, :]) * SCALE + dot(p_low, gl[cols, :])
             total = term if total is None else total + term
-        slot = lax.rem(s, 2)
-        cont[slot] = total.reshape(2, 2, 64, 512)
-        for part in (0, 1):
-            for j in range(4):
-                core_out[s, part, j] = cont[
-                    slot, 1 - c, :, part * 32 : (part + 1) * 32, j * 128 : (j + 1) * 128
-                ].astype(BF16)
-        core_copy(s).start()
+        for n, s in enumerate(steps):
+            slot = s % 4
+            cont[slot] = total[n * 256 : (n + 1) * 256].reshape(2, 2, 64, 512)
+            for part in (0, 1):
+                for j in range(4):
+                    core_out[s, part, j] = cont[
+                        slot, 1 - c, :, part * 32 : (part + 1) * 32, j * 128 : (j + 1) * 128
+                    ].astype(BF16)
+            core_copy(s).start()
 
     def core_sum(s):
         core_copy(s).wait()
-        slot = lax.rem(s, 2)
+        slot = s % 4
         for part in (0, 1):
             for j in range(4):
                 axis_out[s, part, j] = (
@@ -284,34 +305,35 @@
         if not last:
             z_copy(s).start()
 
-    def reduce_step(s, _):
-        contribution(s)
-
-        @pl.when(s >= 1)
-        def _():
-            core_sum(s - 1)
-
-        @pl.when(s >= 1 + LAG)
-        def _():
-            axis_sum(s - 1 - LAG, False)
-
-        return 0
-
-    lax.fori_loop(0, 8, reduce_step, 0)
-
     def query_tile(tile):
-        cols = slice(tile * 256, (tile + 1) * 256)
+        cols = slice(tile * 512, (tile + 1) * 512)
         grad = (dot(keys_t[...], gs_buf[:, cols]) * SCALE).astype(BF16)
-        for i in (0, 1):
-            h = 2 * tile + i
+        for i in range(4):
+            h = 4 * tile + i
             out = dot(ku[h], grad[:, i * 128 : (i + 1) * 128])
             wide[pl.ds(h, 128, stride=8), :] = out.T
 
+    contribution(0)
+    contribution(1, 2)
+    core_sum(0)
+    contribution(3, 4)
+    core_sum(1)
+    core_sum(2)
+    axis_sum(0, False)
+    contribution(5, 6)
+    core_sum(3)
+    core_sum(4)
+    contribution(7)
+    core_sum(5)
+    core_sum(6)
+    axis_sum(1, False)
+    axis_sum(2, False)
     core_sum(7)
+    axis_sum(3, False)
+    axis_sum(4, False)
     query_tile(0)
-    for s in range(7 - LAG, 7):
-        axis_sum(s, False)
-    query_tile(1)
+    axis_sum(5, False)
+    axis_sum(6, False)
     axis_sum(7, True)
     for s in range(7):
         z_copy(s).wait()
@@ -342,8 +364,7 @@
         )
     for copy in first:
         copy.start()
-    query_tile(2)
-    query_tile(3)
+    query_tile(1)
     dq_ref[...] = wide[...].reshape(128, 8, 128).astype(BF16)
     for copy in first:
         copy.wait()
@@ -381,6 +402,11 @@
         dl_ref[32:64, j * 128 : (j + 1) * 128] = last_b[j].astype(F32)
 
 
+def hand_over(dq_in, dl_in, dq_out, dl_out):
+    dq_out[...] = dq_in[...]
+    dl_out[...] = dl_in[...]
+
+
 def on_device(
     latents, queries, grad_out, key_up_matrix, value_up_matrix, parents, branch_node, branch_lengths
 ):
@@ -389,7 +415,7 @@
     anywhere = pl.BlockSpec(memory_space=pl.ANY)
     dma = pltpu.SemaphoreType.DMA
     tile = (2, 32, 128)
-    return pl.pallas_call(
+    d_queries, d_latents = pl.pallas_call(
         kernel,
         name="tree_attention_backward",
         out_shape=(
@@ -404,21 +430,21 @@
             pltpu.VMEM((8, 128, 512), BF16),
             pltpu.VMEM((8, 512, 128), BF16),
             pltpu.VMEM((1024, 128), F32),
-            pltpu.VMEM((8, 2, 2, 64, 512), BF16),
+            pltpu.VMEM((8, 2, 2, 4, 16, 512), BF16),
             pltpu.VMEM((512, 2048), BF16),
             pltpu.VMEM((1024, 512), BF16),
             pltpu.VMEM((1024, 512), BF16),
             pltpu.VMEM((512, 1024), BF16),
             pltpu.VMEM((512, 1024), BF16),
             pltpu.VMEM((256, 128), BF16),
-            pltpu.VMEM((8, 256, 1024), F32),
-            pltpu.VMEM((8, 256, 1024), F32),
+            pltpu.VMEM((8, 2, 2, 64, 1024), F32),
+            pltpu.VMEM((8, 2, 2, 64, 1024), F32),
             pltpu.VMEM((2048, 1024), BF16),
-            pltpu.VMEM((8, 1, 1024), F32),
+            pltpu.VMEM((8, 2, 1, 1024), F32),
             pltpu.VMEM((1, 1024), F32),
             pltpu.VMEM((1, 1024), F32),
             pltpu.VMEM((1, 1024), F32),
-            pltpu.VMEM((2, 2, 2, 64, 512), F32),
+            pltpu.VMEM((4, 2, 2, 64, 512), F32),
             pltpu.VMEM((8, 2, 4) + tile, BF16),
             pltpu.VMEM((8, 2, 4) + tile, BF16),
             pltpu.VMEM((8, 2, 4) + tile, BF16),
@@ -433,9 +459,10 @@
             pltpu.VMEM(tile, BF16),
             pltpu.VMEM(tile, BF16),
             dma((4,)),
-            dma((35,)),
+            dma((73,)),
             dma((1,)),
-            dma((2, 4, 2)),
+            dma((7, 2)),
+            dma((7, 2, 3)),
             dma((8, 2)),
             dma((8,)),
             dma((8,)),
@@ -455,6 +482,16 @@
         latents, parents.reshape(1, 256), branch_node, branch_lengths,
         queries, grad_out, key_up_matrix, value_up_matrix,
     )
+    return pl.pallas_call(
+        hand_over,
+        name="hand_over",
+        out_shape=(
+            jax.ShapeDtypeStruct((128, 8, 128), BF16),
+            jax.ShapeDtypeStruct((64, 512), F32),
+        ),
+        in_specs=[vmem, vmem],
+        out_specs=(vmem, vmem),
+    )(d_queries, d_latents)
 
 
 def solution(mesh):

time: 60.2 us -> 58.2 us (0.967)
  local copies, waits for them, and re-layouts: 2.36 us -> 0 us
    unnamed x4 -> x0, local copies, waits for them, and re-layouts: 2.36 us -> none
    pallas_call x0 -> x1, Pallas kernels: none -> 1.74 us  [on_device(): pl.pallas_call(hand_over, name='hand_over', out_shape=(jax.ShapeDtypeStru...]
    pallas_call x1, Pallas kernels: 56.8 us -> 55.7 us  [on_device(): pl.pallas_call(kernel, name='tree_attention_backward', out_shape=(jax.Sha...]
where the time goes in v2:
time: 58.2 us; the launch traced here: 58 us
  Pallas kernels  57.4 us (99%)
  between operations  0.64 us (1%)
    pallas_call x1, Pallas kernels, on_device(): pl.pallas_call(kernel, name='tree_attention_backward', out_shape=(jax.Sha...  55.7 us
    pallas_call x1, Pallas kernels, on_device(): pl.pallas_call(hand_over, name='hand_over', out_shape=(jax.ShapeDtypeStru...  1.74 us

profile of v2, /device:TPU:2, one launch (start us, length us, event | category | flops | bytes accessed | tf_op | source)
XLA Modules:
  0.0 58.0 jit_solution(32955353745801182)
XLA Ops:
  0.6 55.7 %tree_attention_backward.1 = (bf16[128,8,128]{2,1,0:T(8,128)(2,1)}, f32[64,512]{1,0:T(8,128)}) custom-call(bf16[64,512]{1,0:T(8,128)(2,1)} %lat_ref.1, s32[1,256]{1,0:T(1,128)} %bitcast.1, s32[1,8]{1,0:T(1,128)} %node_ref.1, s32[1,8]{1,0:T(1,128)} %len_ref.1, bf16[128,8,128]{2,1,0:T(8,128)(2,1)} %q_hbm.1, bf16[128,8,128]{2,1,0:T(8,128)(2,1)} %g_hbm.1, ...), custom_call_target="tpu_custom_call" | custom-call | tf_op jit(solution)/shard_map/tree_attention_backward/pallas_call | solution.py:418
  56.3 1.7 %hand_over.1 = (bf16[128,8,128]{2,1,0:T(8,128)(2,1)}, f32[64,512]{1,0:T(8,128)}) custom-call(bf16[128,8,128]{2,1,0:T(8,128)(2,1)} %get-tuple-element.4.dq_in, f32[64,512]{1,0:T(8,128)} %get-tuple-element.5.dl_in), custom_call_target="tpu_custom_call" | custom-call | tf_op jit(solution)/shard_map/hand_over/pallas_call | solution.py:485

commit v3 on v2

--- a/solution.py
+++ b/solution.py
@@ -34,9 +34,9 @@
 
 
 def kernel(
-    lat_ref, par_ref, node_ref, len_ref, q_hbm, g_hbm, ku_hbm, vu_hbm,
+    lat_hbm, par_hbm, node_hbm, len_hbm, q_hbm, g_hbm, ku_hbm, vu_hbm,
     dq_ref, dl_ref,
-    q_in, g_in, ku, vu, wide, keys, keys_t, ql, gl, ql_t, gl_t, live_t,
+    lat_ref, par_ref, node_ref, len_ref, q_in, g_in, ku, vu, wide, keys, keys_t, ql, gl, ql_t, gl_t, live_t,
     w_buf, gw_buf, gs_buf, m_grp, m_run, l_run, d_run,
     cont, core_out, core_in, axis_out, axis_in, z_out, z_in, z_own,
     sum_a, sum_b, last_a, last_b, out_a, out_b,
@@ -52,9 +52,13 @@
     sibling = device(x, y, z, 1 - c)
     partner = device(3 - x, y, z, c)
 
+    pairs = (
+        (lat_hbm, lat_ref), (q_hbm, q_in), (ku_hbm, ku), (g_hbm, g_in), (vu_hbm, vu),
+        (par_hbm, par_ref), (node_hbm, node_ref), (len_hbm, len_ref),
+    )
     loads = [
         pltpu.make_async_copy(src, dst, in_sem.at[i])
-        for i, (src, dst) in enumerate(((q_hbm, q_in), (ku_hbm, ku), (g_hbm, g_in), (vu_hbm, vu)))
+        for i, (src, dst) in enumerate(pairs)
     ]
     for load in loads:
         load.start()
@@ -64,6 +68,7 @@
     peers += [at(k, 0, 0) for k in (1, 2, 3)] + [at(0, k, 0) for k in (1, 2, 3)]
     for peer in peers:
         pl.semaphore_signal(barrier, inc=1, device_id=peer, device_id_type=MESH)
+    loads[0].wait()
     keys[z, c, x_hi] = lat_ref[...].reshape(4, 16, 512)
     pl.semaphore_wait(barrier, len(peers))
 
@@ -114,16 +119,16 @@
             out_ref[h * 128 : (h + 1) * 128, :] = low
             out_t_ref[:, h * 128 : (h + 1) * 128] = low.T
 
-    loads[0].wait()
     loads[1].wait()
+    loads[2].wait()
     latents_of(q_in, ku, ql, ql_t, False)
 
     arrived(keys.at[z, c, 1 - x_hi], x_recv.at[0])
     spread_z(1)
     send(keys.at[z, c, 1 - x_hi], c_recv.at[7, 1], sibling)
 
-    loads[2].wait()
     loads[3].wait()
+    loads[4].wait()
     latents_of(g_in, vu, gl, gl_t, True)
 
     def spread_replicas(kind):
@@ -133,6 +138,8 @@
             for i in range(3):
                 send(piece, n_recv.at[k - 1, kind, i], neighbours[i])
 
+    for load in loads[5:]:
+        load.wait()
     above = lax.broadcasted_iota(jnp.int32, (256, 256), 0)
     below = lax.broadcasted_iota(jnp.int32, (256, 256), 1)
     linked = (above == par_ref[...]) | (above == below)
@@ -207,14 +214,16 @@
             planes.append(plane)
         score_blocks(kind, planes)
 
+    score_from(0, (0,))
+    score_from(1, (0,))
     spread_replicas(1)
     complete(0, near_first)
-    score_from(0, (0,) + near_first[:3])
-    complete(1, near_first[:3])
-    score_from(0, near_first[3:])
-    complete(1, near_first[3:])
-    score_from(1, (0,) + near_first[:3])
-    score_from(1, near_first[3:])
+    score_from(0, near_first[:4])
+    complete(1, near_first[:4])
+    score_from(0, near_first[4:])
+    complete(1, near_first[4:])
+    score_from(1, near_first[:4])
+    score_from(1, near_first[4:])
 
     inv = 1.0 / l_run[...]
     l_run[...] = inv
@@ -411,8 +420,6 @@
     latents, queries, grad_out, key_up_matrix, value_up_matrix, parents, branch_node, branch_lengths
 ):
     vmem = pl.BlockSpec(memory_space=pltpu.VMEM)
-    smem = pl.BlockSpec(memory_space=pltpu.SMEM)
-    anywhere = pl.BlockSpec(memory_space=pl.ANY)
     dma = pltpu.SemaphoreType.DMA
     tile = (2, 32, 128)
     d_queries, d_latents = pl.pallas_call(
@@ -422,9 +429,13 @@
             jax.ShapeDtypeStruct((128, 8, 128), BF16),
             jax.ShapeDtypeStruct((64, 512), F32),
         ),
-        in_specs=[vmem, vmem, smem, smem, anywhere, anywhere, anywhere, anywhere],
+        in_specs=[pl.BlockSpec(memory_space=pltpu.HBM)] * 8,
         out_specs=(vmem, vmem),
         scratch_shapes=[
+            pltpu.VMEM((64, 512), BF16),
+            pltpu.VMEM((1, 256), jnp.int32),
+            pltpu.SMEM((1, 8), jnp.int32),
+            pltpu.SMEM((1, 8), jnp.int32),
             pltpu.VMEM((128, 8, 128), BF16),
             pltpu.VMEM((128, 8, 128), BF16),
             pltpu.VMEM((8, 128, 512), BF16),
@@ -458,7 +469,7 @@
             pltpu.VMEM((4, 32, 128), BF16),
             pltpu.VMEM(tile, BF16),
             pltpu.VMEM(tile, BF16),
-            dma((4,)),
+            dma((8,)),
             dma((73,)),
             dma((1,)),
             dma((7, 2)),

time: 58.2 us -> 56.9 us (0.978)
  Pallas kernels: 57.4 us -> 56.2 us
    pallas_call x1, Pallas kernels: 55.7 us -> 54.4 us  [on_device(): pl.pallas_call(kernel, name='tree_attention_backward', out_shape=(jax.Sha...]
where the time goes in v3:
time: 56.9 us; the launch traced here: 56.8 us
  Pallas kernels  56.2 us (99%)
  between operations  0.64 us (1%)
    pallas_call x1, Pallas kernels, on_device(): pl.pallas_call(kernel, name='tree_attention_backward', out_shape=(jax.Sha...  54.4 us
    pallas_call x1, Pallas kernels, on_device(): pl.pallas_call(hand_over, name='hand_over', out_shape=(jax.ShapeDtypeStru...  1.74 us

profile of v3, /device:TPU:2, one launch (start us, length us, event | category | flops | bytes accessed | tf_op | source)
XLA Modules:
  0.0 56.8 jit_solution(1821448886282345532)
XLA Ops:
  0.6 54.4 %tree_attention_backward.1 = (bf16[128,8,128]{2,1,0:T(8,128)(2,1)}, f32[64,512]{1,0:T(8,128)}) custom-call(bf16[64,512]{1,0:T(8,128)(2,1)} %lat_hbm.1, s32[1,256]{1,0:T(1,128)} %bitcast.1, s32[1,8]{1,0:T(1,128)} %node_hbm.1, s32[1,8]{1,0:T(1,128)} %len_hbm.1, bf16[128,8,128]{2,1,0:T(8,128)(2,1)} %q_hbm.1, bf16[128,8,128]{2,1,0:T(8,128)(2,1)} %g_hbm.1, ...), custom_call_target="tpu_custom_call" | custom-call | tf_op jit(solution)/shard_map/tree_attention_backward/pallas_call | solution.py:425
  55.1 1.7 %hand_over.1 = (bf16[128,8,128]{2,1,0:T(8,128)(2,1)}, f32[64,512]{1,0:T(8,128)}) custom-call(bf16[128,8,128]{2,1,0:T(8,128)(2,1)} %get-tuple-element.4.dq_in, f32[64,512]{1,0:T(8,128)} %get-tuple-element.5.dl_in), custom_call_target="tpu_custom_call" | custom-call | tf_op jit(solution)/shard_map/hand_over/pallas_call | solution.py:496

commit v4 on v3

--- a/solution.py
+++ b/solution.py
@@ -52,6 +52,11 @@
     sibling = device(x, y, z, 1 - c)
     partner = device(3 - x, y, z, c)
 
+    barrier = pltpu.get_barrier_semaphore()
+    peers = [sibling] + [at(0, 0, k) for k in range(1, 8)]
+    peers += [at(k, 0, 0) for k in (1, 2, 3)] + [at(0, k, 0) for k in (1, 2, 3)]
+    for peer in peers:
+        pl.semaphore_signal(barrier, inc=1, device_id=peer, device_id_type=MESH)
     pairs = (
         (lat_hbm, lat_ref), (q_hbm, q_in), (ku_hbm, ku), (g_hbm, g_in), (vu_hbm, vu),
         (par_hbm, par_ref), (node_hbm, node_ref), (len_hbm, len_ref),
@@ -62,12 +67,6 @@
     ]
     for load in loads:
         load.start()
-
-    barrier = pltpu.get_barrier_semaphore()
-    peers = [sibling] + [at(0, 0, k) for k in range(1, 8)]
-    peers += [at(k, 0, 0) for k in (1, 2, 3)] + [at(0, k, 0) for k in (1, 2, 3)]
-    for peer in peers:
-        pl.semaphore_signal(barrier, inc=1, device_id=peer, device_id_type=MESH)
     loads[0].wait()
     keys[z, c, x_hi] = lat_ref[...].reshape(4, 16, 512)
     pl.semaphore_wait(barrier, len(peers))

time: 56.9 us -> 56.9 us (level)
  no operation moved by 1% of the time
where the time goes in v4:
time: 56.9 us; the launch traced here: 56.8 us
  Pallas kernels  56.1 us (99%)
  between operations  0.64 us (1%)
    pallas_call x1, Pallas kernels, on_device(): pl.pallas_call(kernel, name='tree_attention_backward', out_shape=(jax.Sha...  54.4 us
    pallas_call x1, Pallas kernels, on_device(): pl.pallas_call(hand_over, name='hand_over', out_shape=(jax.ShapeDtypeStru...  1.74 us

profile of v4, /device:TPU:2, one launch (start us, length us, event | category | flops | bytes accessed | tf_op | source)
XLA Modules:
  0.0 56.8 jit_solution(1071435977963243452)
XLA Ops:
  0.6 54.4 %tree_attention_backward.1 = (bf16[128,8,128]{2,1,0:T(8,128)(2,1)}, f32[64,512]{1,0:T(8,128)}) custom-call(bf16[64,512]{1,0:T(8,128)(2,1)} %lat_hbm.1, s32[1,256]{1,0:T(1,128)} %bitcast.1, s32[1,8]{1,0:T(1,128)} %node_hbm.1, s32[1,8]{1,0:T(1,128)} %len_hbm.1, bf16[128,8,128]{2,1,0:T(8,128)(2,1)} %q_hbm.1, bf16[128,8,128]{2,1,0:T(8,128)(2,1)} %g_hbm.1, ...), custom_call_target="tpu_custom_call" | custom-call | tf_op jit(solution)/shard_map/tree_attention_backward/pallas_call | solution.py:424
  55.0 1.7 %hand_over.1 = (bf16[128,8,128]{2,1,0:T(8,128)(2,1)}, f32[64,512]{1,0:T(8,128)}) custom-call(bf16[128,8,128]{2,1,0:T(8,128)(2,1)} %get-tuple-element.4.dq_in, f32[64,512]{1,0:T(8,128)} %get-tuple-element.5.dl_in), custom_call_target="tpu_custom_call" | custom-call | tf_op jit(solution)/shard_map/hand_over/pallas_call | solution.py:495
